TPU v7x, 256 devices: a whole 4x4x8 slice. The times are simulated.
256 devices in a mesh: rounds: 8 (over z), tiles: 32 (over y, x, core).
Axes of the slice: x: 4, y: 4, z: 8, core: 2. Of those that a mesh axis runs over, the one named last changes fastest.
Arguments:
- syndromes: int32 [8, 2, 8, 64, 64], P(None, None, 'rounds', 'tiles'), may hold values 0 or 1
- labels: int32 [2, 8], P(None, 'rounds'), may hold values from 0 to 1
- stab_gate: bfloat16 [64, 64, 512], P('tiles'), may hold values from -6 to 6
- bit_gate: float32 [512], replicated, may hold values from -6 to 6
- forget_bias: float32 [128], replicated, may hold values from -1 to 4
- conv_weight: bfloat16 [3, 3, 128, 512], replicated, may hold values from -0.375 to 0.375
- query: float32 [128], replicated, may hold values from -12 to 12
- readout_weight: float32 [128], replicated, may hold values from -6 to 6
Outputs:
- grad_conv: float32 [3, 3, 128, 512], replicated
- grad_stab: float32 [64, 64, 512], P('tiles')
- grad_bit: float32 [512], replicated
- grad_forget: float32 [128], replicated
- grad_query: float32 [128], replicated
- grad_readout: float32 [128], replicated
- loss: float32 [], replicated
All inputs are finite; a program needn't handle non-finite values. No bound on the sum of `syndromes` on one device may be relied on, other than what follows from the above.
Results may differ from a plain program's by a relative error of at most 0.014.
Values may be sent and summed in bfloat16 or wider, within the bound.
No kernel may reach another device: no remote copies, remote signals or barrier semaphores. Data moves between devices by JAX's collectives and lax.ppermute only.
A program may use at most 64 MiB of HBM per device.

v0:
```python
import math
import jax
import jax.numpy as jnp
from jax import lax
from jax.sharding import PartitionSpec as P


def with_halo(cells, sides, width):
    for axis, dim in sides:
        count = lax.axis_size(axis)
        ends = count - 1
        head = lax.slice_in_dim(cells, 0, width, axis=dim)
        tail = lax.slice_in_dim(cells, cells.shape[dim] - width, cells.shape[dim], axis=dim)
        cells = jnp.concatenate(
            [
                lax.ppermute(tail, axis, [(i, (i + 1) % count) for i in range(ends)]),
                cells,
                lax.ppermute(head, axis, [((i + 1) % count, i) for i in range(ends)]),
            ],
            axis=dim,
        )
    return cells


def make_patches(padded):
    row_count = padded.shape[1] - 2
    col_count = padded.shape[2] - 2
    pieces = [
        padded[:, a : a + row_count, b : b + col_count, :] for a in range(3) for b in range(3)
    ]
    return jnp.concatenate(pieces, axis=-1).reshape(-1, 9 * padded.shape[3])


def pad_columns(d_field):
    return jnp.pad(d_field, ((0, 0), (0, 0), (1, 1), (0, 0)))


def cell_forward(gate_input, cell_prev, channels):
    input_gate = jax.nn.sigmoid(gate_input[:, :channels])
    forget = jax.nn.sigmoid(gate_input[:, channels : 2 * channels])
    candidate = jnp.tanh(gate_input[:, 2 * channels : 3 * channels])
    output_gate = jax.nn.sigmoid(gate_input[:, 3 * channels :])
    cell_new = forget * cell_prev + input_gate * candidate
    hidden_new = (output_gate * jnp.tanh(cell_new)).astype(jnp.bfloat16)
    gate_values = jnp.concatenate([input_gate, forget, candidate, output_gate], axis=1)
    return (gate_values, cell_new, hidden_new)


def cell_backward(gate_values, cell_prev, cell_new, d_hidden, d_cell, channels):
    input_gate = gate_values[:, :channels]
    forget = gate_values[:, channels : 2 * channels]
    candidate = gate_values[:, 2 * channels : 3 * channels]
    output_gate = gate_values[:, 3 * channels :]
    squash = jnp.tanh(cell_new)
    d_total = d_cell + d_hidden * output_gate * (1.0 - squash * squash)
    d_gates = jnp.concatenate(
        [
            d_total * candidate * input_gate * (1.0 - input_gate),
            d_total * cell_prev * forget * (1.0 - forget),
            d_total * input_gate * (1.0 - candidate * candidate),
            d_hidden * squash * output_gate * (1.0 - output_gate),
        ],
        axis=1,
    ).astype(jnp.bfloat16)
    return (d_gates, d_total * forget)


def column_total(products, col_count, row_shift):
    result = products[:, :, 2 : 2 + col_count, row_shift, 0]
    for col_shift in range(1, 3):
        result = (
            result + products[:, :, 2 - col_shift : 2 - col_shift + col_count, row_shift, col_shift]
        )
    return result


def transpose_products(d_field, weight_matrix, channels):
    products = lax.dot_general(
        d_field, weight_matrix, (((3,), (1,)), ((), ())), preferred_element_type=jnp.float32
    )
    return products.reshape(d_field.shape[:3] + (3, 3, channels))


def per_device(
    syndromes, labels, stab_gate, bit_gate, forget_bias, conv_weight, query, readout_weight
):
    round_count, micro_count, shot_count, tile_rows, columns = syndromes.shape
    channels = conv_weight.shape[2]
    gate_units = conv_weight.shape[3]
    tile_sites = tile_rows * columns
    flat_rows = shot_count * tile_sites
    weight_matrix = conv_weight.reshape(9 * channels, gate_units)
    stab_rows = stab_gate.reshape(1, tile_sites, gate_units).astype(jnp.float32)
    forget_shift = jnp.concatenate(
        [jnp.zeros((channels,), jnp.float32), forget_bias, jnp.zeros((2 * channels,), jnp.float32)]
    )
    score_scale = 1.0 / math.sqrt(channels)
    field_shape = (shot_count, tile_rows, columns, channels)
    gate_shape = (shot_count, tile_rows, columns, gate_units)
    lead_tile = (lax.axis_index("tiles") == 0).astype(jnp.float32)

    def forward_round(recurrent, fired_bits):
        hidden_prev, cell_prev = recurrent
        hidden_rows = with_halo(hidden_prev, (("tiles", 1),), 1)
        hidden_pad = pad_columns(hidden_rows)
        gate_input = jnp.dot(
            make_patches(hidden_pad), weight_matrix, preferred_element_type=jnp.float32
        )
        gate_input = (
            gate_input.reshape(shot_count, tile_sites, gate_units)
            + stab_rows
            + fired_bits.astype(jnp.float32).reshape(shot_count, tile_sites, 1) * bit_gate
            + forget_shift
        )
        gate_values, cell_new, hidden_new = cell_forward(
            gate_input.reshape(flat_rows, gate_units), cell_prev, channels
        )
        return (
            (hidden_new.reshape(field_shape), cell_new),
            (hidden_pad, gate_values, cell_prev, cell_new, fired_bits),
        )

    def backward_round(state_carry, saved_items):
        d_hidden, d_cell, grad_weight, grad_stab_part, grad_fired, grad_keep = state_carry
        hidden_pad, gate_values, cell_prev, cell_new, fired_bits = saved_items
        d_gates, d_cell_prev = cell_backward(
            gate_values, cell_prev, cell_new, d_hidden, d_cell, channels
        )
        grad_weight = grad_weight + lax.dot_general(
            make_patches(hidden_pad),
            d_gates,
            (((0,), (0,)), ((), ())),
            preferred_element_type=jnp.float32,
        )
        grad_stab_part = grad_stab_part + jnp.sum(
            d_gates.reshape(shot_count, tile_sites, gate_units).astype(jnp.float32), axis=0
        )
        fired_row = fired_bits.astype(jnp.bfloat16).reshape(1, flat_rows)
        grad_fired = grad_fired + jnp.dot(fired_row, d_gates, preferred_element_type=jnp.float32)[0]
        grad_keep = grad_keep + jnp.sum(
            d_gates[:, channels : 2 * channels].astype(jnp.float32), axis=0
        )
        d_field = d_gates.reshape(gate_shape)
        d_rows = with_halo(d_field, (("tiles", 1),), 1)
        products = transpose_products(pad_columns(d_rows), weight_matrix, channels)
        d_hidden_prev = column_total(products[:, 2 : 2 + tile_rows], columns, 0)
        for row_shift in range(1, 3):
            d_hidden_prev = d_hidden_prev + column_total(
                products[:, 2 - row_shift : 2 - row_shift + tile_rows], columns, row_shift
            )
        return (
            (
                d_hidden_prev.reshape(flat_rows, channels),
                d_cell_prev,
                grad_weight,
                grad_stab_part,
                grad_fired,
                grad_keep,
            ),
            None,
        )

    def one_batch(totals, inputs):
        fired_rounds, batch_labels = inputs
        initial = (
            jnp.zeros(field_shape, jnp.bfloat16),
            jnp.zeros((flat_rows, channels), jnp.float32),
        )
        (hidden_last, unused_cell), saved = lax.scan(forward_round, initial, fired_rounds)
        hidden_full = hidden_last.astype(jnp.float32).reshape(shot_count, tile_sites, channels)
        scores = jnp.sum(hidden_full * query, axis=2) * score_scale
        exp_score = jnp.exp(scores)
        part_total = jnp.sum(exp_score, axis=1)
        part_numer = jnp.sum(exp_score[..., None] * hidden_full, axis=1)
        total_exp, numer = lax.psum((part_total, part_numer), "tiles")
        pooled = numer / total_exp[:, None]
        logit_value = jnp.sum(pooled * readout_weight, axis=1)
        targets = batch_labels.astype(jnp.float32)
        loss_part = jnp.sum(jax.nn.softplus(logit_value) - targets * logit_value)
        d_logit = jax.nn.sigmoid(logit_value) - targets
        d_pooled = d_logit[:, None] * readout_weight
        weight = exp_score / total_exp[:, None]
        d_score = weight * (
            jnp.sum(hidden_full * d_pooled[:, None, :], axis=2)
            - jnp.sum(pooled * d_pooled, axis=1)[:, None]
        )
        final_grad = (
            weight[..., None] * d_pooled[:, None, :] + d_score[..., None] * query * score_scale
        )
        query_part = score_scale * jnp.sum(d_score[..., None] * hidden_full, axis=(0, 1))
        readout_part = jnp.sum(d_logit[:, None] * pooled, axis=0)
        grad_weight, grad_stab_part, grad_fired, grad_keep, grad_query, grad_readout, loss_total = (
            totals
        )
        start_back = (
            final_grad.reshape(flat_rows, channels),
            jnp.zeros((flat_rows, channels), jnp.float32),
            grad_weight,
            grad_stab_part,
            grad_fired,
            grad_keep,
        )
        back_state, unused_out = lax.scan(backward_round, start_back, saved, reverse=True)
        return (
            (
                back_state[2],
                back_state[3],
                back_state[4],
                back_state[5],
                grad_query + query_part,
                grad_readout + readout_part,
                loss_total + loss_part,
            ),
            None,
        )

    zero_totals = (
        jnp.zeros((9 * channels, gate_units), jnp.float32),
        jnp.zeros((tile_sites, gate_units), jnp.float32),
        jnp.zeros((gate_units,), jnp.float32),
        jnp.zeros((channels,), jnp.float32),
        jnp.zeros((channels,), jnp.float32),
        jnp.zeros((channels,), jnp.float32),
        jnp.zeros((), jnp.float32),
    )
    batch_inputs = (jnp.swapaxes(syndromes, 0, 1), labels)
    sums, unused_out = lax.scan(one_batch, zero_totals, batch_inputs)
    grad_weight, grad_stab_part, grad_fired, grad_keep, grad_query, grad_readout, loss_total = sums
    stab_total = lax.psum(grad_stab_part.astype(jnp.bfloat16), "rounds").astype(jnp.float32)
    totals = lax.psum(
        (
            grad_weight,
            grad_fired,
            grad_keep,
            grad_query,
            grad_readout * lead_tile,
            loss_total * lead_tile,
        ),
        ("rounds", "tiles"),
    )
    return (
        totals[0].reshape(3, 3, channels, gate_units),
        stab_total.reshape(tile_rows, columns, gate_units),
        totals[1],
        totals[2],
        totals[3],
        totals[4],
        totals[5],
    )


def solution(mesh):
    in_specs = (
        P(None, None, "rounds", "tiles", None),
        P(None, "rounds"),
        P("tiles", None, None),
        P(),
        P(),
        P(),
        P(),
        P(),
    )
    out_specs = (P(), P("tiles", None, None), P(), P(), P(), P(), P())
    return jax.shard_map(
        per_device, mesh=mesh, in_specs=in_specs, out_specs=out_specs, check_vma=False
    )
```

profile of v0, /device:TPU:2, one launch (start us, length us, event | category | flops | bytes accessed | tf_op | source)
XLA Modules:
  0.0 1043.6 jit_solution(17618227137616668080)
XLA Ops:
  11.9 661.5 %while.108 = (s32[]{:T(128)}, f32[1152,512]{1,0:T(8,128)S(1)}, f32[128,512]{1,0:T(8,128)}, f32[512]{0:T(512)S(1)}, f32[128]{0:T(128)}, /*index=5*/f32[128]{0:T(1...) while((s32[]{:T(128)}, f32[1152,512]{1,0:T(8,128)S(1)}, ...), condition=%wide.region_15.16_spmd.clone, body=%wide.region_0.15_spmd.clone.sunk | while | flops 621755008 | bytes 24381452 | solution.py:227
  13.2 88.8 %while.109 = (s32[]{:T(128)}, bf16[1,2,64,128]{3,2,1,0:T(8,128)(2,1)S(1)}, f32[128,128]{1,0:T(8,128)S(1)}, bf16[8,1,4,66,128]{4,3,2,1,0:T(8,128)(2,1)}, f32[8,12...) while((s32[]{:T(128)}, ...), condition=%wide.region_2.2_spmd.clone, body=%wide.region_1.1_spmd.clone.sunk | while | flops 152739968 | bytes 4702967 | solution.py:169
  103.6 68.7 %all-reduce.5 = (f32[]{:T(128)}, f32[1,128]{1,0:T(1,128)S(1)}) all-reduce(f32[]{:T(128)} %get-tuple-element.1439, f32[1,128]{1,0:T(1,128)S(1)} %bitcast.186), channel_id=1, replica_groups=mesh['rounds'=8,'tiles'=32] {'tiles'}, use_global_device_ids=true, to_apply=%region_5.5 | all-reduce | flops 129 | bytes 1032 | tf_op jit(solution)/shard_map/while/body/eval_jaxpr/psum | solution.py:175
  185.9 148.6 %while.110 = (s32[]{:T(128)}, f32[128,128]{1,0:T(8,128)S(1)}, f32[128,128]{1,0:T(8,128)}, f32[1152,512]{1,0:T(8,128)S(1)}, f32[128,512]{1,0:T(8,128)}, /*index=5...) while((s32[]{:T(128)}, f32[128,128]{1,0:T(8,128)S(1)}, ...), condition=%wide.region_13.13_spmd.clone, body=%wide.region_11.12_spmd.clone.sunk | while | flops 468750976 | bytes 19420224 | solution.py:203
  189.8 6.0 collective-permute-start.2
  228.7 3.6 collective-permute-start.2
  301.9 3.6 collective-permute-start.2
  335.8 100.8 %while.109 = (s32[]{:T(128)}, bf16[1,2,64,128]{3,2,1,0:T(8,128)(2,1)S(1)}, f32[128,128]{1,0:T(8,128)S(1)}, bf16[8,1,4,66,128]{4,3,2,1,0:T(8,128)(2,1)}, f32[8,12...) while((s32[]{:T(128)}, ...), condition=%wide.region_2.2_spmd.clone, body=%wide.region_1.1_spmd.clone.sunk | while | flops 152739968 | bytes 4702967 | solution.py:169
  335.9 3.6 collective-permute-start
  350.5 4.8 collective-permute-start.1
  362.1 5.8 collective-permute-start.1
  374.6 5.8 collective-permute-start.1
  387.2 5.8 collective-permute-start.1
  399.7 5.8 collective-permute-start.1
  412.3 6.3 collective-permute-start.1
  425.4 6.3 collective-permute-start.1
  438.3 72.4 %all-reduce.5 = (f32[]{:T(128)}, f32[1,128]{1,0:T(1,128)S(1)}) all-reduce(f32[]{:T(128)} %get-tuple-element.1439, f32[1,128]{1,0:T(1,128)S(1)} %bitcast.186), channel_id=1, replica_groups=mesh['rounds'=8,'tiles'=32] {'tiles'}, use_global_device_ids=true, to_apply=%region_5.5 | all-reduce | flops 129 | bytes 1032 | tf_op jit(solution)/shard_map/while/body/eval_jaxpr/psum | solution.py:175
  524.8 148.6 %while.110 = (s32[]{:T(128)}, f32[128,128]{1,0:T(8,128)S(1)}, f32[128,128]{1,0:T(8,128)}, f32[1152,512]{1,0:T(8,128)S(1)}, f32[128,512]{1,0:T(8,128)}, /*index=5...) while((s32[]{:T(128)}, f32[128,128]{1,0:T(8,128)S(1)}, ...), condition=%wide.region_13.13_spmd.clone, body=%wide.region_11.12_spmd.clone.sunk | while | flops 468750976 | bytes 19420224 | solution.py:203
  528.7 6.0 collective-permute-start.2
  585.9 3.6 collective-permute-start.2
  604.2 3.6 collective-permute-start.2
  640.8 3.6 collective-permute-start.2
  676.7 94.3 %all-reduce.3 = (f32[512]{0:T(512)}, f32[128]{0:T(128)}, f32[128]{0:T(128)}, f32[128]{0:T(128)}, f32[]{:T(128)}) all-reduce(f32[512]{0:T(512)S(1)} %get-tuple-element.1688, f32[128]{0:T(128)S(1)} %copy-done.13, f32[128]{0:T(128)} %get-tuple-element.1690, ...), channel_id=1, replica_groups=mesh['rounds'=8,'tiles'=32] {'rounds','tiles'}, use_global_device_ids=true, to_apply=%region_18.19 | all-reduce | flops 897 | bytes 7176 | tf_op jit(solution)/shard_map/psum | solution.py:230
  772.7 260.7 %all-reduce.9.cloned.1.call-done = f32[3,3,128,512]{3,2,1,0:T(8,128)} async-done(((f32[3,3,128,512]{3,2,1,0:T(8,128)}), f32[3,3,128,512]{3,2,1,0:T(8,128)}) %all-reduce.9.cloned.1.call-update) | async-done | bytes 2359312 | tf_op jit(solution)/shard_map/psum | solution.py:230
  (1210 shorter events, 443.5 us)
Async XLA Ops:
  7.2 763.9 %all-reduce.11.cloned.1.call-start = ((), (), s32[]{:S(2)}) async-start(), calls=%async_computation.1 | async-start | bytes 262144 | tf_op jit(solution)/shard_map/psum | solution.py:229
  189.8 15.2 %collective-permute-start.2 = (bf16[1,1,64,512]{3,2,1,0:T(8,128)(2,1)}, bf16[1,1,64,512]{3,2,1,0:T(8,128)(2,1)}, u32[]{:S(2)}, u32[]{:S(2)}) collective-permute-start(bf16[1,1,64,512]{3,2,1,0:T(8,128)(2,1)} %get-tuple-element.1494), channel_id=1, source_target_pairs={{1,0},{2,1},{3,2},{4,3},{5,4},{6,5},{7,6},{8,7},{9,8},{10,9},{11,1... | collective-permute-start | bytes 196616 | tf_op jit(solution)/shard_map/while/body/eval_jaxpr/while/body/eval_jaxpr/ppermute | solution.py:18
  210.5 12.8 %collective-permute-start.2 = (bf16[1,1,64,512]{3,2,1,0:T(8,128)(2,1)}, bf16[1,1,64,512]{3,2,1,0:T(8,128)(2,1)}, u32[]{:S(2)}, u32[]{:S(2)}) collective-permute-start(bf16[1,1,64,512]{3,2,1,0:T(8,128)(2,1)} %get-tuple-element.1494), channel_id=1, source_target_pairs={{1,0},{2,1},{3,2},{4,3},{5,4},{6,5},{7,6},{8,7},{9,8},{10,9},{11,1... | collective-permute-start | bytes 196616 | tf_op jit(solution)/shard_map/while/body/eval_jaxpr/while/body/eval_jaxpr/ppermute | solution.py:18
  228.7 12.9 %collective-permute-start.2 = (bf16[1,1,64,512]{3,2,1,0:T(8,128)(2,1)}, bf16[1,1,64,512]{3,2,1,0:T(8,128)(2,1)}, u32[]{:S(2)}, u32[]{:S(2)}) collective-permute-start(bf16[1,1,64,512]{3,2,1,0:T(8,128)(2,1)} %get-tuple-element.1494), channel_id=1, source_target_pairs={{1,0},{2,1},{3,2},{4,3},{5,4},{6,5},{7,6},{8,7},{9,8},{10,9},{11,1... | collective-permute-start | bytes 196616 | tf_op jit(solution)/shard_map/while/body/eval_jaxpr/while/body/eval_jaxpr/ppermute | solution.py:18
  232.4 9.2 collective-permute-start.3
  247.1 12.8 %collective-permute-start.2 = (bf16[1,1,64,512]{3,2,1,0:T(8,128)(2,1)}, bf16[1,1,64,512]{3,2,1,0:T(8,128)(2,1)}, u32[]{:S(2)}, u32[]{:S(2)}) collective-permute-start(bf16[1,1,64,512]{3,2,1,0:T(8,128)(2,1)} %get-tuple-element.1494), channel_id=1, source_target_pairs={{1,0},{2,1},{3,2},{4,3},{5,4},{6,5},{7,6},{8,7},{9,8},{10,9},{11,1... | collective-permute-start | bytes 196616 | tf_op jit(solution)/shard_map/while/body/eval_jaxpr/while/body/eval_jaxpr/ppermute | solution.py:18
  265.3 12.8 %collective-permute-start.2 = (bf16[1,1,64,512]{3,2,1,0:T(8,128)(2,1)}, bf16[1,1,64,512]{3,2,1,0:T(8,128)(2,1)}, u32[]{:S(2)}, u32[]{:S(2)}) collective-permute-start(bf16[1,1,64,512]{3,2,1,0:T(8,128)(2,1)} %get-tuple-element.1494), channel_id=1, source_target_pairs={{1,0},{2,1},{3,2},{4,3},{5,4},{6,5},{7,6},{8,7},{9,8},{10,9},{11,1... | collective-permute-start | bytes 196616 | tf_op jit(solution)/shard_map/while/body/eval_jaxpr/while/body/eval_jaxpr/ppermute | solution.py:18
  283.6 12.8 %collective-permute-start.2 = (bf16[1,1,64,512]{3,2,1,0:T(8,128)(2,1)}, bf16[1,1,64,512]{3,2,1,0:T(8,128)(2,1)}, u32[]{:S(2)}, u32[]{:S(2)}) collective-permute-start(bf16[1,1,64,512]{3,2,1,0:T(8,128)(2,1)} %get-tuple-element.1494), channel_id=1, source_target_pairs={{1,0},{2,1},{3,2},{4,3},{5,4},{6,5},{7,6},{8,7},{9,8},{10,9},{11,1... | collective-permute-start | bytes 196616 | tf_op jit(solution)/shard_map/while/body/eval_jaxpr/while/body/eval_jaxpr/ppermute | solution.py:18
  287.2 9.2 collective-permute-start.3
  301.9 12.8 %collective-permute-start.2 = (bf16[1,1,64,512]{3,2,1,0:T(8,128)(2,1)}, bf16[1,1,64,512]{3,2,1,0:T(8,128)(2,1)}, u32[]{:S(2)}, u32[]{:S(2)}) collective-permute-start(bf16[1,1,64,512]{3,2,1,0:T(8,128)(2,1)} %get-tuple-element.1494), channel_id=1, source_target_pairs={{1,0},{2,1},{3,2},{4,3},{5,4},{6,5},{7,6},{8,7},{9,8},{10,9},{11,1... | collective-permute-start | bytes 196616 | tf_op jit(solution)/shard_map/while/body/eval_jaxpr/while/body/eval_jaxpr/ppermute | solution.py:18
  320.1 12.8 %collective-permute-start.2 = (bf16[1,1,64,512]{3,2,1,0:T(8,128)(2,1)}, bf16[1,1,64,512]{3,2,1,0:T(8,128)(2,1)}, u32[]{:S(2)}, u32[]{:S(2)}) collective-permute-start(bf16[1,1,64,512]{3,2,1,0:T(8,128)(2,1)} %get-tuple-element.1494), channel_id=1, source_target_pairs={{1,0},{2,1},{3,2},{4,3},{5,4},{6,5},{7,6},{8,7},{9,8},{10,9},{11,1... | collective-permute-start | bytes 196616 | tf_op jit(solution)/shard_map/while/body/eval_jaxpr/while/body/eval_jaxpr/ppermute | solution.py:18
  528.7 15.2 %collective-permute-start.2 = (bf16[1,1,64,512]{3,2,1,0:T(8,128)(2,1)}, bf16[1,1,64,512]{3,2,1,0:T(8,128)(2,1)}, u32[]{:S(2)}, u32[]{:S(2)}) collective-permute-start(bf16[1,1,64,512]{3,2,1,0:T(8,128)(2,1)} %get-tuple-element.1494), channel_id=1, source_target_pairs={{1,0},{2,1},{3,2},{4,3},{5,4},{6,5},{7,6},{8,7},{9,8},{10,9},{11,1... | collective-permute-start | bytes 196616 | tf_op jit(solution)/shard_map/while/body/eval_jaxpr/while/body/eval_jaxpr/ppermute | solution.py:18
  534.7 9.2 collective-permute-start.3
  549.4 12.8 %collective-permute-start.2 = (bf16[1,1,64,512]{3,2,1,0:T(8,128)(2,1)}, bf16[1,1,64,512]{3,2,1,0:T(8,128)(2,1)}, u32[]{:S(2)}, u32[]{:S(2)}) collective-permute-start(bf16[1,1,64,512]{3,2,1,0:T(8,128)(2,1)} %get-tuple-element.1494), channel_id=1, source_target_pairs={{1,0},{2,1},{3,2},{4,3},{5,4},{6,5},{7,6},{8,7},{9,8},{10,9},{11,1... | collective-permute-start | bytes 196616 | tf_op jit(solution)/shard_map/while/body/eval_jaxpr/while/body/eval_jaxpr/ppermute | solution.py:18
  553.0 9.2 collective-permute-start.3
  567.6 12.8 %collective-permute-start.2 = (bf16[1,1,64,512]{3,2,1,0:T(8,128)(2,1)}, bf16[1,1,64,512]{3,2,1,0:T(8,128)(2,1)}, u32[]{:S(2)}, u32[]{:S(2)}) collective-permute-start(bf16[1,1,64,512]{3,2,1,0:T(8,128)(2,1)} %get-tuple-element.1494), channel_id=1, source_target_pairs={{1,0},{2,1},{3,2},{4,3},{5,4},{6,5},{7,6},{8,7},{9,8},{10,9},{11,1... | collective-permute-start | bytes 196616 | tf_op jit(solution)/shard_map/while/body/eval_jaxpr/while/body/eval_jaxpr/ppermute | solution.py:18
  571.3 9.2 collective-permute-start.3
  585.9 12.8 %collective-permute-start.2 = (bf16[1,1,64,512]{3,2,1,0:T(8,128)(2,1)}, bf16[1,1,64,512]{3,2,1,0:T(8,128)(2,1)}, u32[]{:S(2)}, u32[]{:S(2)}) collective-permute-start(bf16[1,1,64,512]{3,2,1,0:T(8,128)(2,1)} %get-tuple-element.1494), channel_id=1, source_target_pairs={{1,0},{2,1},{3,2},{4,3},{5,4},{6,5},{7,6},{8,7},{9,8},{10,9},{11,1... | collective-permute-start | bytes 196616 | tf_op jit(solution)/shard_map/while/body/eval_jaxpr/while/body/eval_jaxpr/ppermute | solution.py:18
  604.2 12.8 %collective-permute-start.2 = (bf16[1,1,64,512]{3,2,1,0:T(8,128)(2,1)}, bf16[1,1,64,512]{3,2,1,0:T(8,128)(2,1)}, u32[]{:S(2)}, u32[]{:S(2)}) collective-permute-start(bf16[1,1,64,512]{3,2,1,0:T(8,128)(2,1)} %get-tuple-element.1494), channel_id=1, source_target_pairs={{1,0},{2,1},{3,2},{4,3},{5,4},{6,5},{7,6},{8,7},{9,8},{10,9},{11,1... | collective-permute-start | bytes 196616 | tf_op jit(solution)/shard_map/while/body/eval_jaxpr/while/body/eval_jaxpr/ppermute | solution.py:18
  622.5 12.8 %collective-permute-start.2 = (bf16[1,1,64,512]{3,2,1,0:T(8,128)(2,1)}, bf16[1,1,64,512]{3,2,1,0:T(8,128)(2,1)}, u32[]{:S(2)}, u32[]{:S(2)}) collective-permute-start(bf16[1,1,64,512]{3,2,1,0:T(8,128)(2,1)} %get-tuple-element.1494), channel_id=1, source_target_pairs={{1,0},{2,1},{3,2},{4,3},{5,4},{6,5},{7,6},{8,7},{9,8},{10,9},{11,1... | collective-permute-start | bytes 196616 | tf_op jit(solution)/shard_map/while/body/eval_jaxpr/while/body/eval_jaxpr/ppermute | solution.py:18
  626.1 9.2 collective-permute-start.3
  640.8 12.8 %collective-permute-start.2 = (bf16[1,1,64,512]{3,2,1,0:T(8,128)(2,1)}, bf16[1,1,64,512]{3,2,1,0:T(8,128)(2,1)}, u32[]{:S(2)}, u32[]{:S(2)}) collective-permute-start(bf16[1,1,64,512]{3,2,1,0:T(8,128)(2,1)} %get-tuple-element.1494), channel_id=1, source_target_pairs={{1,0},{2,1},{3,2},{4,3},{5,4},{6,5},{7,6},{8,7},{9,8},{10,9},{11,1... | collective-permute-start | bytes 196616 | tf_op jit(solution)/shard_map/while/body/eval_jaxpr/while/body/eval_jaxpr/ppermute | solution.py:18
  659.0 12.8 %collective-permute-start.2 = (bf16[1,1,64,512]{3,2,1,0:T(8,128)(2,1)}, bf16[1,1,64,512]{3,2,1,0:T(8,128)(2,1)}, u32[]{:S(2)}, u32[]{:S(2)}) collective-permute-start(bf16[1,1,64,512]{3,2,1,0:T(8,128)(2,1)} %get-tuple-element.1494), channel_id=1, source_target_pairs={{1,0},{2,1},{3,2},{4,3},{5,4},{6,5},{7,6},{8,7},{9,8},{10,9},{11,1... | collective-permute-start | bytes 196616 | tf_op jit(solution)/shard_map/while/body/eval_jaxpr/while/body/eval_jaxpr/ppermute | solution.py:18
  675.3 358.1 %all-reduce.9.cloned.1.call-start = ((), (), s32[]{:S(2)}) async-start(), calls=%async_computation | async-start | bytes 4718592 | tf_op jit(solution)/shard_map/psum | solution.py:230
  (222 other events, 1132.7 us)
Sparse Core Ops, SparseCore 0:
  675.4 90.3 all-reduce.10
  771.8 261.6 all-reduce.8
where the time goes:
time: 1050 us; the launch traced here: 1040 us
  waiting for transfers between devices  279 us (27%)
  blocking collectives  235 us (22%)
  starting transfers between devices  189 us (18%)
  other arithmetic  168 us (16%)
  matrix products  77.6 us (7%)
  local copies, waits for them, and re-layouts  65.3 us (6%)
  loops' own time  15.4 us (1%)
  between operations  14.1 us (1%)
    psum x1, waiting for transfers between devices, per_device(): lax.psum((grad_weight, grad_fired, grad_keep, grad_query, grad_readout *...  261 us
    psum x2, blocking collectives, one_batch(): total_exp, numer = lax.psum((part_total, part_numer), 'tiles')  141 us
    ppermute x32, starting transfers between devices, with_halo(): lax.ppermute(head, axis, [((i + 1) % count, i) for i in range(ends)])  95.1 us
    psum x1, blocking collectives, per_device(): lax.psum((grad_weight, grad_fired, grad_keep, grad_query, grad_readout *...  94.3 us
    ppermute x32, starting transfers between devices, with_halo(): lax.ppermute(tail, axis, [(i, (i + 1) % count) for i in range(ends)])  93.7 us
    dynamic_update_slice x48, other arithmetic, one_batch(): lax.scan(forward_round, initial, fired_rounds)  33.1 us
    squeeze x32, local copies, waits for them, and re-layouts, one_batch(): lax.scan(backward_round, start_back, saved, reverse=True)  29.9 us
    add x16, other arithmetic, backward_round(): grad_stab_part + jnp.sum(d_gates.reshape(shot_count, tile_sites, gate_uni...  28.7 us
  transfers between devices with their start and end apart: 66, of which 15 were waited for; matrix products, arithmetic and copies ran while one was open for 12% of the time, Pallas kernels for 0%

commit v1 on v0

--- a/solution.py
+++ b/solution.py
@@ -228,15 +228,18 @@
     grad_weight, grad_stab_part, grad_fired, grad_keep, grad_query, grad_readout, loss_total = sums
     stab_total = lax.psum(grad_stab_part.astype(jnp.bfloat16), "rounds").astype(jnp.float32)
     totals = lax.psum(
-        (
-            grad_weight,
-            grad_fired,
-            grad_keep,
-            grad_query,
-            grad_readout * lead_tile,
-            loss_total * lead_tile,
+        lax.psum(
+            (
+                grad_weight,
+                grad_fired,
+                grad_keep,
+                grad_query,
+                grad_readout * lead_tile,
+                loss_total * lead_tile,
+            ),
+            "tiles",
         ),
-        ("rounds", "tiles"),
+        "rounds",
     )
     return (
         totals[0].reshape(3, 3, channels, gate_units),

time: 1050 us -> 987 us (0.940)
  waiting for transfers between devices: 279 us -> 227 us
  blocking collectives: 235 us -> 222 us
    psum x1, waiting for transfers between devices: 261 us -> 133 us  [per_device(): lax.psum((grad_weight, grad_fired, grad_keep, grad_query, grad_readout *...]
    psum x0 -> x1, waiting for transfers between devices: none -> 76.9 us  [per_device(): lax.psum(lax.psum((grad_weight, grad_fired, grad_keep, grad_query, grad_r...]
    psum x1, blocking collectives: 94.3 us -> 62.4 us  [per_device(): lax.psum((grad_weight, grad_fired, grad_keep, grad_query, grad_readout *...]
    psum x0 -> x1, blocking collectives: none -> 18.1 us  [per_device(): lax.psum(lax.psum((grad_weight, grad_fired, grad_keep, grad_query, grad_r...]
  transfers between devices with their start and end apart: 66 -> 67, of which waited for: 15 -> 17; matrix products, arithmetic and copies ran while one was open for 12% -> 13% of each run, Pallas kernels for 0% -> 0%
where the time goes in v1:
time: 987 us; the launch traced here: 980 us
  waiting for transfers between devices  227 us (23%)
  blocking collectives  222 us (22%)
  starting transfers between devices  189 us (19%)
  other arithmetic  167 us (17%)
  matrix products  77.6 us (8%)
  local copies, waits for them, and re-layouts  66.7 us (7%)
  loops' own time  17.1 us (2%)
  between operations  13.8 us (1%)
    psum x2, blocking collectives, one_batch(): total_exp, numer = lax.psum((part_total, part_numer), 'tiles')  141 us
    psum x1, waiting for transfers between devices, per_device(): lax.psum((grad_weight, grad_fired, grad_keep, grad_query, grad_readout *...  133 us
    ppermute x32, starting transfers between devices, with_halo(): lax.ppermute(head, axis, [((i + 1) % count, i) for i in range(ends)])  95.2 us
    ppermute x32, starting transfers between devices, with_halo(): lax.ppermute(tail, axis, [(i, (i + 1) % count) for i in range(ends)])  93.7 us
    psum x1, waiting for transfers between devices, per_device(): lax.psum(lax.psum((grad_weight, grad_fired, grad_keep, grad_query, grad_r...  76.9 us
    psum x1, blocking collectives, per_device(): lax.psum((grad_weight, grad_fired, grad_keep, grad_query, grad_readout *...  62.4 us
    dynamic_update_slice x48, other arithmetic, one_batch(): lax.scan(forward_round, initial, fired_rounds)  33.1 us
    squeeze x32, local copies, waits for them, and re-layouts, one_batch(): lax.scan(backward_round, start_back, saved, reverse=True)  29.9 us
  transfers between devices with their start and end apart: 67, of which 17 were waited for; matrix products, arithmetic and copies ran while one was open for 13% of the time, Pallas kernels for 0%

profile of v1, /device:TPU:2, one launch (start us, length us, event | category | flops | bytes accessed | tf_op | source)
XLA Modules:
  0.0 980.3 jit_solution(2812449524779749377)
XLA Ops:
  11.9 662.5 %while.108 = (s32[]{:T(128)}, f32[1152,512]{1,0:T(8,128)S(1)}, f32[128,512]{1,0:T(8,128)}, f32[512]{0:T(512)S(1)}, f32[128]{0:T(128)}, /*index=5*/f32[128]{0:T(1...) while((s32[]{:T(128)}, f32[1152,512]{1,0:T(8,128)S(1)}, ...), condition=%wide.region_15.16_spmd.clone, body=%wide.region_0.15_spmd.clone.sunk | while | flops 621755008 | bytes 24381452 | solution.py:227
  13.2 88.8 %while.109 = (s32[]{:T(128)}, bf16[1,2,64,128]{3,2,1,0:T(8,128)(2,1)S(1)}, f32[128,128]{1,0:T(8,128)S(1)}, bf16[8,1,4,66,128]{4,3,2,1,0:T(8,128)(2,1)}, f32[8,12...) while((s32[]{:T(128)}, ...), condition=%wide.region_2.2_spmd.clone, body=%wide.region_1.1_spmd.clone.sunk | while | flops 152739968 | bytes 4702967 | solution.py:169
  103.6 68.7 %all-reduce.6 = (f32[]{:T(128)}, f32[1,128]{1,0:T(1,128)S(1)}) all-reduce(f32[]{:T(128)} %get-tuple-element.1444, f32[1,128]{1,0:T(1,128)S(1)} %bitcast.186), channel_id=1, replica_groups=mesh['rounds'=8,'tiles'=32] {'tiles'}, use_global_device_ids=true, to_apply=%region_5.5 | all-reduce | flops 129 | bytes 1032 | tf_op jit(solution)/shard_map/while/body/eval_jaxpr/psum | solution.py:175
  186.5 148.4 %while.110 = (s32[]{:T(128)}, f32[128,128]{1,0:T(8,128)S(1)}, f32[128,128]{1,0:T(8,128)}, f32[1152,512]{1,0:T(8,128)S(1)}, f32[128,512]{1,0:T(8,128)}, /*index=5...) while((s32[]{:T(128)}, f32[128,128]{1,0:T(8,128)S(1)}, ...), condition=%wide.region_13.13_spmd.clone, body=%wide.region_11.12_spmd.clone.sunk | while | flops 468750976 | bytes 19420224 | solution.py:203
  190.4 6.0 collective-permute-start.2
  229.3 3.6 collective-permute-start.2
  247.6 3.6 collective-permute-start.2
  336.3 100.8 %while.109 = (s32[]{:T(128)}, bf16[1,2,64,128]{3,2,1,0:T(8,128)(2,1)S(1)}, f32[128,128]{1,0:T(8,128)S(1)}, bf16[8,1,4,66,128]{4,3,2,1,0:T(8,128)(2,1)}, f32[8,12...) while((s32[]{:T(128)}, ...), condition=%wide.region_2.2_spmd.clone, body=%wide.region_1.1_spmd.clone.sunk | while | flops 152739968 | bytes 4702967 | solution.py:169
  336.3 3.6 collective-permute-start
  351.0 4.8 collective-permute-start.1
  362.5 5.7 collective-permute-start.1
  375.1 5.8 collective-permute-start.1
  387.7 5.7 collective-permute-start.1
  400.2 5.8 collective-permute-start.1
  412.8 6.4 collective-permute-start.1
  425.9 6.3 collective-permute-start.1
  438.7 72.4 %all-reduce.6 = (f32[]{:T(128)}, f32[1,128]{1,0:T(1,128)S(1)}) all-reduce(f32[]{:T(128)} %get-tuple-element.1444, f32[1,128]{1,0:T(1,128)S(1)} %bitcast.186), channel_id=1, replica_groups=mesh['rounds'=8,'tiles'=32] {'tiles'}, use_global_device_ids=true, to_apply=%region_5.5 | all-reduce | flops 129 | bytes 1032 | tf_op jit(solution)/shard_map/while/body/eval_jaxpr/psum | solution.py:175
  525.9 148.4 %while.110 = (s32[]{:T(128)}, f32[128,128]{1,0:T(8,128)S(1)}, f32[128,128]{1,0:T(8,128)}, f32[1152,512]{1,0:T(8,128)S(1)}, f32[128,512]{1,0:T(8,128)}, /*index=5...) while((s32[]{:T(128)}, f32[128,128]{1,0:T(8,128)S(1)}, ...), condition=%wide.region_13.13_spmd.clone, body=%wide.region_11.12_spmd.clone.sunk | while | flops 468750976 | bytes 19420224 | solution.py:203
  529.8 6.0 collective-permute-start.2
  568.6 3.6 collective-permute-start.2
  677.5 133.1 %all-reduce.11.cloned.1.call-done = f32[1152,512]{1,0:T(8,128)} async-done(((f32[1152,512]{1,0:T(8,128)}), f32[1152,512]{1,0:T(8,128)}) %all-reduce.11.cloned.1.call-update) | async-done | bytes 2359312 | tf_op jit(solution)/shard_map/psum | solution.py:231
  811.3 62.4 %all-reduce.3 = (f32[512]{0:T(512)S(1)}, f32[128]{0:T(128)S(1)}, f32[128]{0:T(128)S(1)}, f32[128]{0:T(128)S(1)}, f32[]{:T(128)}) all-reduce(f32[512]{0:T(512)S(1)} %get-tuple-element.1697, f32[128]{0:T(128)S(1)} %copy-done.13, f32[128]{0:T(128)} %get-tuple-element.1699, ...), channel_id=1, replica_groups=mesh['rounds'=8,'tiles'=32] {'tiles'}, use_global_device_ids=true, to_apply=%region_19.20 | all-reduce | flops 897 | bytes 7176 | tf_op jit(solution)/shard_map/psum | solution.py:231
  873.7 18.1 %all-reduce.4 = (f32[512]{0:T(512)}, f32[128]{0:T(128)}, f32[128]{0:T(128)}, f32[128]{0:T(128)}, f32[]{:T(128)}) all-reduce(f32[512]{0:T(512)S(1)} %get-tuple-element.1090, f32[128]{0:T(128)S(1)} %get-tuple-element.1091, f32[128]{0:T(128)S(1)} %get-tuple-element.1092, ...), channel_id=1, replica_groups=mesh['rounds'=8,'tiles'=32] {'rounds'}, use_global_device_ids=true, to_apply=%region_20.21 | all-reduce | flops 897 | bytes 7176 | tf_op jit(solution)/shard_map/psum | solution.py:230
  893.5 76.9 %all-reduce.13.cloned.1.call-done = f32[3,3,128,512]{3,2,1,0:T(8,128)} async-done(((f32[3,3,128,512]{3,2,1,0:T(8,128)}), f32[3,3,128,512]{3,2,1,0:T(8,128)}) %all-reduce.13.cloned.1.call-update) | async-done | bytes 2359312 | tf_op jit(solution)/shard_map/psum | solution.py:230
  (1214 shorter events, 450.7 us)
Async XLA Ops:
  7.2 803.5 %all-reduce.11.cloned.1.call-start = ((), (), s32[]{:S(2)}) async-start(), calls=%async_computation | async-start | bytes 4718592 | tf_op jit(solution)/shard_map/psum | solution.py:231
  190.4 15.2 %collective-permute-start.2 = (bf16[1,1,64,512]{3,2,1,0:T(8,128)(2,1)}, bf16[1,1,64,512]{3,2,1,0:T(8,128)(2,1)}, u32[]{:S(2)}, u32[]{:S(2)}) collective-permute-start(bf16[1,1,64,512]{3,2,1,0:T(8,128)(2,1)} %get-tuple-element.1499), channel_id=1, source_target_pairs={{1,0},{2,1},{3,2},{4,3},{5,4},{6,5},{7,6},{8,7},{9,8},{10,9},{11,1... | collective-permute-start | bytes 196616 | tf_op jit(solution)/shard_map/while/body/eval_jaxpr/while/body/eval_jaxpr/ppermute | solution.py:18
  196.4 9.2 collective-permute-start.3
  211.0 12.8 %collective-permute-start.2 = (bf16[1,1,64,512]{3,2,1,0:T(8,128)(2,1)}, bf16[1,1,64,512]{3,2,1,0:T(8,128)(2,1)}, u32[]{:S(2)}, u32[]{:S(2)}) collective-permute-start(bf16[1,1,64,512]{3,2,1,0:T(8,128)(2,1)} %get-tuple-element.1499), channel_id=1, source_target_pairs={{1,0},{2,1},{3,2},{4,3},{5,4},{6,5},{7,6},{8,7},{9,8},{10,9},{11,1... | collective-permute-start | bytes 196616 | tf_op jit(solution)/shard_map/while/body/eval_jaxpr/while/body/eval_jaxpr/ppermute | solution.py:18
  229.3 12.9 %collective-permute-start.2 = (bf16[1,1,64,512]{3,2,1,0:T(8,128)(2,1)}, bf16[1,1,64,512]{3,2,1,0:T(8,128)(2,1)}, u32[]{:S(2)}, u32[]{:S(2)}) collective-permute-start(bf16[1,1,64,512]{3,2,1,0:T(8,128)(2,1)} %get-tuple-element.1499), channel_id=1, source_target_pairs={{1,0},{2,1},{3,2},{4,3},{5,4},{6,5},{7,6},{8,7},{9,8},{10,9},{11,1... | collective-permute-start | bytes 196616 | tf_op jit(solution)/shard_map/while/body/eval_jaxpr/while/body/eval_jaxpr/ppermute | solution.py:18
  232.9 9.2 collective-permute-start.3
  247.6 12.8 %collective-permute-start.2 = (bf16[1,1,64,512]{3,2,1,0:T(8,128)(2,1)}, bf16[1,1,64,512]{3,2,1,0:T(8,128)(2,1)}, u32[]{:S(2)}, u32[]{:S(2)}) collective-permute-start(bf16[1,1,64,512]{3,2,1,0:T(8,128)(2,1)} %get-tuple-element.1499), channel_id=1, source_target_pairs={{1,0},{2,1},{3,2},{4,3},{5,4},{6,5},{7,6},{8,7},{9,8},{10,9},{11,1... | collective-permute-start | bytes 196616 | tf_op jit(solution)/shard_map/while/body/eval_jaxpr/while/body/eval_jaxpr/ppermute | solution.py:18
  265.8 12.8 %collective-permute-start.2 = (bf16[1,1,64,512]{3,2,1,0:T(8,128)(2,1)}, bf16[1,1,64,512]{3,2,1,0:T(8,128)(2,1)}, u32[]{:S(2)}, u32[]{:S(2)}) collective-permute-start(bf16[1,1,64,512]{3,2,1,0:T(8,128)(2,1)} %get-tuple-element.1499), channel_id=1, source_target_pairs={{1,0},{2,1},{3,2},{4,3},{5,4},{6,5},{7,6},{8,7},{9,8},{10,9},{11,1... | collective-permute-start | bytes 196616 | tf_op jit(solution)/shard_map/while/body/eval_jaxpr/while/body/eval_jaxpr/ppermute | solution.py:18
  284.0 12.8 %collective-permute-start.2 = (bf16[1,1,64,512]{3,2,1,0:T(8,128)(2,1)}, bf16[1,1,64,512]{3,2,1,0:T(8,128)(2,1)}, u32[]{:S(2)}, u32[]{:S(2)}) collective-permute-start(bf16[1,1,64,512]{3,2,1,0:T(8,128)(2,1)} %get-tuple-element.1499), channel_id=1, source_target_pairs={{1,0},{2,1},{3,2},{4,3},{5,4},{6,5},{7,6},{8,7},{9,8},{10,9},{11,1... | collective-permute-start | bytes 196616 | tf_op jit(solution)/shard_map/while/body/eval_jaxpr/while/body/eval_jaxpr/ppermute | solution.py:18
  302.3 12.8 %collective-permute-start.2 = (bf16[1,1,64,512]{3,2,1,0:T(8,128)(2,1)}, bf16[1,1,64,512]{3,2,1,0:T(8,128)(2,1)}, u32[]{:S(2)}, u32[]{:S(2)}) collective-permute-start(bf16[1,1,64,512]{3,2,1,0:T(8,128)(2,1)} %get-tuple-element.1499), channel_id=1, source_target_pairs={{1,0},{2,1},{3,2},{4,3},{5,4},{6,5},{7,6},{8,7},{9,8},{10,9},{11,1... | collective-permute-start | bytes 196616 | tf_op jit(solution)/shard_map/while/body/eval_jaxpr/while/body/eval_jaxpr/ppermute | solution.py:18
  320.6 12.9 %collective-permute-start.2 = (bf16[1,1,64,512]{3,2,1,0:T(8,128)(2,1)}, bf16[1,1,64,512]{3,2,1,0:T(8,128)(2,1)}, u32[]{:S(2)}, u32[]{:S(2)}) collective-permute-start(bf16[1,1,64,512]{3,2,1,0:T(8,128)(2,1)} %get-tuple-element.1499), channel_id=1, source_target_pairs={{1,0},{2,1},{3,2},{4,3},{5,4},{6,5},{7,6},{8,7},{9,8},{10,9},{11,1... | collective-permute-start | bytes 196616 | tf_op jit(solution)/shard_map/while/body/eval_jaxpr/while/body/eval_jaxpr/ppermute | solution.py:18
  324.2 9.2 collective-permute-start.3
  529.8 15.2 %collective-permute-start.2 = (bf16[1,1,64,512]{3,2,1,0:T(8,128)(2,1)}, bf16[1,1,64,512]{3,2,1,0:T(8,128)(2,1)}, u32[]{:S(2)}, u32[]{:S(2)}) collective-permute-start(bf16[1,1,64,512]{3,2,1,0:T(8,128)(2,1)} %get-tuple-element.1499), channel_id=1, source_target_pairs={{1,0},{2,1},{3,2},{4,3},{5,4},{6,5},{7,6},{8,7},{9,8},{10,9},{11,1... | collective-permute-start | bytes 196616 | tf_op jit(solution)/shard_map/while/body/eval_jaxpr/while/body/eval_jaxpr/ppermute | solution.py:18
  550.4 12.8 %collective-permute-start.2 = (bf16[1,1,64,512]{3,2,1,0:T(8,128)(2,1)}, bf16[1,1,64,512]{3,2,1,0:T(8,128)(2,1)}, u32[]{:S(2)}, u32[]{:S(2)}) collective-permute-start(bf16[1,1,64,512]{3,2,1,0:T(8,128)(2,1)} %get-tuple-element.1499), channel_id=1, source_target_pairs={{1,0},{2,1},{3,2},{4,3},{5,4},{6,5},{7,6},{8,7},{9,8},{10,9},{11,1... | collective-permute-start | bytes 196616 | tf_op jit(solution)/shard_map/while/body/eval_jaxpr/while/body/eval_jaxpr/ppermute | solution.py:18
  568.6 12.9 %collective-permute-start.2 = (bf16[1,1,64,512]{3,2,1,0:T(8,128)(2,1)}, bf16[1,1,64,512]{3,2,1,0:T(8,128)(2,1)}, u32[]{:S(2)}, u32[]{:S(2)}) collective-permute-start(bf16[1,1,64,512]{3,2,1,0:T(8,128)(2,1)} %get-tuple-element.1499), channel_id=1, source_target_pairs={{1,0},{2,1},{3,2},{4,3},{5,4},{6,5},{7,6},{8,7},{9,8},{10,9},{11,1... | collective-permute-start | bytes 196616 | tf_op jit(solution)/shard_map/while/body/eval_jaxpr/while/body/eval_jaxpr/ppermute | solution.py:18
  572.3 9.2 collective-permute-start.3
  586.9 12.8 %collective-permute-start.2 = (bf16[1,1,64,512]{3,2,1,0:T(8,128)(2,1)}, bf16[1,1,64,512]{3,2,1,0:T(8,128)(2,1)}, u32[]{:S(2)}, u32[]{:S(2)}) collective-permute-start(bf16[1,1,64,512]{3,2,1,0:T(8,128)(2,1)} %get-tuple-element.1499), channel_id=1, source_target_pairs={{1,0},{2,1},{3,2},{4,3},{5,4},{6,5},{7,6},{8,7},{9,8},{10,9},{11,1... | collective-permute-start | bytes 196616 | tf_op jit(solution)/shard_map/while/body/eval_jaxpr/while/body/eval_jaxpr/ppermute | solution.py:18
  605.2 12.8 %collective-permute-start.2 = (bf16[1,1,64,512]{3,2,1,0:T(8,128)(2,1)}, bf16[1,1,64,512]{3,2,1,0:T(8,128)(2,1)}, u32[]{:S(2)}, u32[]{:S(2)}) collective-permute-start(bf16[1,1,64,512]{3,2,1,0:T(8,128)(2,1)} %get-tuple-element.1499), channel_id=1, source_target_pairs={{1,0},{2,1},{3,2},{4,3},{5,4},{6,5},{7,6},{8,7},{9,8},{10,9},{11,1... | collective-permute-start | bytes 196616 | tf_op jit(solution)/shard_map/while/body/eval_jaxpr/while/body/eval_jaxpr/ppermute | solution.py:18
  623.4 12.8 %collective-permute-start.2 = (bf16[1,1,64,512]{3,2,1,0:T(8,128)(2,1)}, bf16[1,1,64,512]{3,2,1,0:T(8,128)(2,1)}, u32[]{:S(2)}, u32[]{:S(2)}) collective-permute-start(bf16[1,1,64,512]{3,2,1,0:T(8,128)(2,1)} %get-tuple-element.1499), channel_id=1, source_target_pairs={{1,0},{2,1},{3,2},{4,3},{5,4},{6,5},{7,6},{8,7},{9,8},{10,9},{11,1... | collective-permute-start | bytes 196616 | tf_op jit(solution)/shard_map/while/body/eval_jaxpr/while/body/eval_jaxpr/ppermute | solution.py:18
  641.7 12.8 %collective-permute-start.2 = (bf16[1,1,64,512]{3,2,1,0:T(8,128)(2,1)}, bf16[1,1,64,512]{3,2,1,0:T(8,128)(2,1)}, u32[]{:S(2)}, u32[]{:S(2)}) collective-permute-start(bf16[1,1,64,512]{3,2,1,0:T(8,128)(2,1)} %get-tuple-element.1499), channel_id=1, source_target_pairs={{1,0},{2,1},{3,2},{4,3},{5,4},{6,5},{7,6},{8,7},{9,8},{10,9},{11,1... | collective-permute-start | bytes 196616 | tf_op jit(solution)/shard_map/while/body/eval_jaxpr/while/body/eval_jaxpr/ppermute | solution.py:18
  660.0 12.9 %collective-permute-start.2 = (bf16[1,1,64,512]{3,2,1,0:T(8,128)(2,1)}, bf16[1,1,64,512]{3,2,1,0:T(8,128)(2,1)}, u32[]{:S(2)}, u32[]{:S(2)}) collective-permute-start(bf16[1,1,64,512]{3,2,1,0:T(8,128)(2,1)} %get-tuple-element.1499), channel_id=1, source_target_pairs={{1,0},{2,1},{3,2},{4,3},{5,4},{6,5},{7,6},{8,7},{9,8},{10,9},{11,1... | collective-permute-start | bytes 196616 | tf_op jit(solution)/shard_map/while/body/eval_jaxpr/while/body/eval_jaxpr/ppermute | solution.py:18
  663.6 9.2 collective-permute-start.3
  675.8 216.1 %all-reduce.15.cloned.1.call-start = ((), (), s32[]{:S(2)}) async-start(), calls=%async_computation.2 | async-start | bytes 262144 | tf_op jit(solution)/shard_map/psum | solution.py:229
  677.5 293.0 %all-reduce.13.cloned.1.call-start = ((), (), s32[]{:S(2)}) async-start(), calls=%async_computation.1 | async-start | bytes 4718592 | tf_op jit(solution)/shard_map/psum | solution.py:230
  (223 other events, 1274.7 us)
Sparse Core Ops, SparseCore 0:
  675.9 134.6 all-reduce.10
  813.0 72.8 all-reduce.14
  888.3 82.1 all-reduce.12
